TPU v7x, 512 devices: a whole 4x4x16 slice. The times are simulated.
512 devices in a mesh: seq: 64 (over z, y), head: 8 (over x, core).
Axes of the slice: x: 4, y: 4, z: 16, core: 2. Of those that a mesh axis runs over, the one named last changes fastest.
Arguments:
- query_rows: bfloat16 [16384, 4096], P('seq', 'head'), may hold values from -5.5 to 5.5
- key_rows: bfloat16 [16384, 4096], P('seq', 'head'), may hold values from -5.5 to 5.5
- value_rows: bfloat16 [16384, 4096], P('seq', 'head'), may hold values from -6 to 6
- cluster_ids: int32 [16, 16384, 1], P('head', 'seq'), may hold values from 0 to 255; in each aligned block of 256 rows (0 to 255, 256 to 511, ..., all dimensions but the last counted through in order) at most 2 rows name the same one
Outputs:
- attended: bfloat16 [16384, 4096], P('seq', 'head')
Inputs may be any that keep to these rules, and one draw needn't show every extreme that they name: `cluster_ids`: for each routing head, the 256 tokens of one index of seq name any one cluster at most 2 times, and some cluster exactly that often.
All inputs are finite; a program needn't handle non-finite values.
Results may differ from a plain program's by a relative error of at most 0.0045.
Values may be sent and summed in bfloat16 or wider, within the bound.
A program may use at most 64 MiB of HBM per device.

v0:
```python
import math

import jax
import jax.numpy as jnp
from jax import lax
from jax.sharding import PartitionSpec as P

CLUSTERS = 256
WINDOW = 1024
SRC_CAP = 2


NEG_FILL = -1e30


def shifted(value, axis, steps):
    count = lax.axis_size(axis)
    initial, last = (max(0, -steps), min(count, count - steps))
    return lax.ppermute(value, axis, [(source, source + steps) for source in range(initial, last)])


def blend_rows(scores, allowed, value_block, einsum_form):
    scores = jnp.where(allowed, scores, NEG_FILL)
    largest = jnp.max(scores, axis=-1, keepdims=True)
    raised = jnp.exp(scores - largest)
    weights = (raised / jnp.sum(raised, axis=-1, keepdims=True)).astype(jnp.bfloat16)
    return jnp.einsum(einsum_form, weights, value_block, preferred_element_type=jnp.float32).astype(
        jnp.bfloat16
    )


def cluster_attend(query_part, key_part, value_part, slot_pos, head_width):
    sources, groups, owned, slot_room = slot_pos.shape
    capacity = sources * slot_room

    def regroup(tensor):
        return tensor.transpose(1, 2, 0, 3, 4).reshape(groups, owned, capacity, tensor.shape[-1])

    query_group = regroup(query_part)
    key_group = regroup(key_part)
    value_group = regroup(value_part)
    where_at = slot_pos.transpose(1, 2, 0, 3).reshape(groups, owned, capacity)
    allowed = (where_at[:, :, None, :] <= where_at[:, :, :, None]) & (where_at[:, :, None, :] >= 0)
    scores = jnp.einsum(
        "hcqd,hckd->hcqk", query_group, key_group, preferred_element_type=jnp.float32
    ) * (1.0 / math.sqrt(head_width))
    mixed = blend_rows(scores, allowed, value_group, "hcqk,hckd->hcqd")
    return mixed.reshape(groups, owned, sources, slot_room, head_width).transpose(2, 0, 1, 3, 4)


def per_device(query_rows, key_rows, value_rows, cluster_ids):
    tok_rows = query_rows.shape[0]
    pair = cluster_ids.shape[0]
    head_width = query_rows.shape[1] // (2 * pair)
    split = pair * head_width
    place = lax.axis_index("seq")
    seq_count = lax.axis_size("seq")
    scale = 1.0 / math.sqrt(head_width)
    local_q = query_rows[:, :split].reshape(tok_rows, pair, head_width)
    local_k = key_rows[:, :split].reshape(tok_rows, pair, head_width)
    local_v = value_rows[:, :split].reshape(tok_rows, pair, head_width)
    span = (WINDOW + tok_rows - 2) // tok_rows
    earlier_k = []
    earlier_v = []
    for offset in range(span, 0, -1):
        moved_k, moved_v = shifted((local_k, local_v), "seq", offset)
        earlier_k.append(moved_k)
        earlier_v.append(moved_v)
    every_k = jnp.concatenate(earlier_k + [local_k], 0)
    every_v = jnp.concatenate(earlier_v + [local_v], 0)
    key_pos = (place - span) * tok_rows + jnp.arange((span + 1) * tok_rows, dtype=jnp.int32)
    block = min(tok_rows, 512)

    def local_block(index):
        start = index * block
        query_pos = place * tok_rows + start + jnp.arange(block, dtype=jnp.int32)
        allowed = (
            (key_pos[None, :] <= query_pos[:, None])
            & (key_pos[None, :] > query_pos[:, None] - WINDOW)
            & (key_pos[None, :] >= 0)
        )
        scores = (
            jnp.einsum("qhd,khd->hqk", local_q, every_k, preferred_element_type=jnp.float32) * scale
        )
        return blend_rows(scores, allowed[None], every_v, "hqk,khd->qhd")

    local_out = lax.map(local_block, jnp.arange(tok_rows // block, dtype=jnp.int32)).reshape(
        tok_rows, split
    )
    owned = CLUSTERS // seq_count
    slot_room = SRC_CAP
    cluster_now = cluster_ids[:, :, 0]
    onehot = (cluster_now[:, :, None] == jnp.arange(CLUSTERS, dtype=jnp.int32)).astype(jnp.int32)
    rank = jnp.sum(jnp.cumsum(onehot, axis=1) * onehot, axis=-1) - 1
    per_dest = pair * owned * slot_room
    target = (
        cluster_now // owned * per_dest
        + jnp.arange(pair, dtype=jnp.int32)[:, None] * (owned * slot_room)
        + cluster_now % owned * slot_room
        + rank
    )
    target = target.reshape(-1)
    token_pos = jnp.broadcast_to(
        place * tok_rows + jnp.arange(tok_rows, dtype=jnp.int32), (pair, tok_rows)
    ).reshape(-1)
    send_pos = (
        jnp.full((seq_count * per_dest,), -1, jnp.int32)
        .at[target]
        .set(token_pos)
        .reshape(seq_count, pair, owned, slot_room)
    )

    def heads_first(matrix):
        return (
            matrix[:, split:]
            .reshape(tok_rows, pair, head_width)
            .transpose(1, 0, 2)
            .reshape(pair * tok_rows, head_width)
        )

    def packed(columns):
        stacked = jnp.concatenate(columns, -1)
        span_cols = stacked.shape[-1]
        filled = jnp.zeros((seq_count * per_dest, span_cols), jnp.bfloat16).at[target].set(stacked)
        return filled.reshape(seq_count, pair, owned, slot_room, span_cols)

    pairs_in, pos_in = (
        lax.all_to_all(
            packed([heads_first(key_rows), heads_first(value_rows)]),
            "seq",
            split_axis=0,
            concat_axis=0,
            tiled=True,
        ),
        lax.all_to_all(send_pos, "seq", split_axis=0, concat_axis=0, tiled=True),
    )
    query_in = lax.all_to_all(
        packed([heads_first(query_rows)]), "seq", split_axis=0, concat_axis=0, tiled=True
    )
    mixed = cluster_attend(
        query_in, pairs_in[..., :head_width], pairs_in[..., head_width:], pos_in, head_width
    )
    home = lax.all_to_all(mixed, "seq", split_axis=0, concat_axis=0, tiled=True).reshape(
        seq_count * per_dest, head_width
    )
    routed = (
        home[target].reshape(pair, tok_rows, head_width).transpose(1, 0, 2).reshape(tok_rows, split)
    )
    return jnp.concatenate([local_out, routed], 1)


def solution(mesh):
    in_specs = (P("seq", "head"), P("seq", "head"), P("seq", "head"), P("head", "seq", None))
    out_specs = P("seq", "head")
    return jax.shard_map(
        per_device, mesh=mesh, in_specs=in_specs, out_specs=out_specs, check_vma=False
    )
```

profile of v0, /device:TPU:6, one launch (start us, length us, event | category | flops | bytes accessed | tf_op | source)
XLA Modules:
  0.0 153.1 jit_solution(7561700372277620999)
XLA Ops:
  0.0 0.7 copy.112
  0.7 0.8 copy.74
  1.5 0.4 fusion.11
  2.0 0.2 broadcast_add_fusion
  2.2 0.0 copy-start.3
  2.3 0.0 copy-start
  2.3 0.2 fusion.12
  2.5 0.1 broadcast_bitcast_fusion.1
  2.6 0.3 copy-done.3
  2.9 2.4 %scatter_custom_fusion = s32[1024]{0:T(1024)S(1)} fusion(s32[512]{0:T(512)S(1)} %bitcast.121, s32[512]{0:T(512)S(1)} %bitcast.127, s32[]{:T(128)} %constant.83.clone.1), kind=kCustom, calls=%fused_computation.68 | custom fusion | bytes 4100 | tf_op jit(solution)/shard_map/scatter | solution.py:109
  5.4 0.3 reshape.327
  5.7 1.5 copy.76
  7.2 18.7 %all-to-all-start = ((s32[64,2,4,2]{2,3,1,0:T(2,128)}), s32[64,2,4,2]{2,3,1,0:T(2,128)S(1)}, u32[]{:S(2)}, u32[]{:S(2)}) async-start(s32[64,2,4,2]{2,3,1,0:T(2,128)} %copy.76), calls=%async_computation | async-start | bytes 262144 | tf_op jit(solution)/shard_map/all_to_all | solution.py:135
  26.0 0.0 copy-start.1
  26.0 0.1 copy.100
  26.1 0.1 copy.82
  26.2 2.4 %scatter_custom_fusion.1 = bf16[1024,128]{1,0:T(8,128)(2,1)} fusion(s32[512]{0:T(512)S(1)} %bitcast.122, bf16[512,128]{1,0:T(8,128)(2,1)S(1)} %bitcast.117, bf16[]{:T(256)} %constant.91.clone.1), kind=kCustom, calls=%fused_computation.40 | custom fusion | bytes 262146 | tf_op jit(solution)/shard_map/scatter | solution.py:124
  28.6 15.0 %all-to-all-done = s32[64,2,4,2]{2,3,1,0:T(2,128)S(1)} async-done(((s32[64,2,4,2]{2,3,1,0:T(2,128)}), s32[64,2,4,2]{2,3,1,0:T(2,128)S(1)}, u32[]{:S(2)}, u32[]{:S(2)}) %all-to-all-start) | async-done | bytes 4128 | tf_op jit(solution)/shard_map/all_to_all | solution.py:135
  43.6 4.6 %all-to-all-start.1 = ((bf16[64,2,4,2,128]{4,3,2,1,0:T(2,128)(2,1)}), bf16[64,2,4,2,128]{4,3,2,1,0:T(2,128)(2,1)S(1)}, u32[]{:S(2)}, u32[]{:S(2)}) async-start(bf16[64,2,4,2,128]{4,3,2,1,0:T(2,128)(2,1)} %bitcast.17), calls=%async_computation.1 | async-start | bytes 524288 | tf_op jit(solution)/shard_map/all_to_all | solution.py:137
  48.2 0.0 copy-start.2
  48.3 0.1 copy.102
  48.4 0.1 copy.87
  48.5 0.7 copy-done.2
  49.2 0.1 copy.101
  49.3 0.1 copy.85
  49.4 2.5 %scatter_custom_fusion.2 = bf16[1024,256]{1,0:T(8,128)(2,1)S(1)} fusion(s32[512]{0:T(512)S(1)} %bitcast.123, bf16[512,128]{1,0:T(8,128)(2,1)S(1)} %bitcast.107, bf16[]{:T(256)} %constant.93, bf16[512,128]{1,0:T(8,128)(2,1)S(1)} %bitcast.108, bf16[]{:T(256)} %constant.91.clone.1), kind=kCustom, calls=%fused_computation.29 | custom fusion | flops 524288 | bytes 786436 | tf_op jit(solution)/shard_map/scatter | solution.py:124
  51.9 1.0 reshape.336
  52.9 17.0 %all-to-all-done.1 = bf16[64,2,4,2,128]{4,3,2,1,0:T(2,128)(2,1)S(1)} async-done(((bf16[64,2,4,2,128]{4,3,2,1,0:T(2,128)(2,1)}), bf16[64,2,4,2,128]{4,3,2,1,0:T(2,128)(2,1)S(1)}, u32[]{:S(2)}, u32[]{:S(2)}) %all-to-all-start.1) | async-done | bytes 262176 | tf_op jit(solution)/shard_map/all_to_all | solution.py:137
  69.9 4.7 %all-to-all-start.2 = ((bf16[64,2,4,2,256]{4,3,2,1,0:T(2,128)(2,1)}), bf16[64,2,4,2,256]{4,3,2,1,0:T(2,128)(2,1)S(1)}, u32[]{:S(2)}, u32[]{:S(2)}) async-start(bf16[64,2,4,2,256]{4,3,2,1,0:T(2,128)(2,1)} %reshape.336), calls=%async_computation.2 | async-start | bytes 1048576 | tf_op jit(solution)/shard_map/all_to_all | solution.py:128
  74.7 0.1 copy.64
  74.8 3.5 %collective-permute-start = (bf16[256,2,128]{0,2,1:T(8,128)(2,1)S(1)}, bf16[256,2,128]{0,2,1:T(8,128)(2,1)S(1)}, u32[]{:S(2)}, u32[]{:S(2)}) collective-permute-start(bf16[256,2,128]{0,2,1:T(8,128)(2,1)S(1)} %bitcast.98), channel_id=1, source_target_pairs={{0,32},{8,40},{16,48},{24,56},{32,64},{40,72},{48,80},{56,88},{64,... | collective-permute-start | bytes 393224 | tf_op jit(solution)/shard_map/ppermute | solution.py:19
  78.2 4.6 %collective-permute-start.1 = (bf16[256,2,128]{0,2,1:T(8,128)(2,1)S(1)}, bf16[256,2,128]{0,2,1:T(8,128)(2,1)S(1)}, u32[]{:S(2)}, u32[]{:S(2)}) collective-permute-start(bf16[256,2,128]{0,2,1:T(8,128)(2,1)S(1)} %bitcast.99), channel_id=1, source_target_pairs={{0,24},{8,32},{16,40},{24,48},{32,56},{40,64},{48,72},{56,80},{64,... | collective-permute-start | bytes 393224 | tf_op jit(solution)/shard_map/ppermute | solution.py:19
  82.8 3.7 %collective-permute-start.2 = (bf16[256,2,128]{0,2,1:T(8,128)(2,1)S(1)}, bf16[256,2,128]{0,2,1:T(8,128)(2,1)S(1)}, u32[]{:S(2)}, u32[]{:S(2)}) collective-permute-start(bf16[256,2,128]{0,2,1:T(8,128)(2,1)S(1)} %bitcast.100), channel_id=1, source_target_pairs={{0,16},{8,24},{16,32},{24,40},{32,48},{40,56},{48,64},{56,72},{64,... | collective-permute-start | bytes 393224 | tf_op jit(solution)/shard_map/ppermute | solution.py:19
  86.5 2.8 %collective-permute-start.3 = (bf16[256,2,128]{0,2,1:T(8,128)(2,1)S(1)}, bf16[256,2,128]{0,2,1:T(8,128)(2,1)S(1)}, u32[]{:S(2)}, u32[]{:S(2)}) collective-permute-start(bf16[256,2,128]{0,2,1:T(8,128)(2,1)S(1)} %bitcast.101), channel_id=1, source_target_pairs={{0,8},{8,16},{16,24},{24,32},{32,40},{40,48},{48,56},{56,64},{64,7... | collective-permute-start | bytes 393224 | tf_op jit(solution)/shard_map/ppermute | solution.py:19
  89.3 0.1 copy.98
  89.4 0.1 copy.66
  89.5 3.4 %collective-permute-start.4 = (bf16[256,2,128]{2,0,1:T(8,128)(2,1)S(1)}, bf16[256,2,128]{2,0,1:T(8,128)(2,1)S(1)}, u32[]{:S(2)}, u32[]{:S(2)}) collective-permute-start(bf16[256,2,128]{2,0,1:T(8,128)(2,1)S(1)} %copy.66), channel_id=1, source_target_pairs={{0,32},{8,40},{16,48},{24,56},{32,64},{40,72},{48,80},{56,88},{64,... | collective-permute-start | bytes 393224 | tf_op jit(solution)/shard_map/ppermute | solution.py:19
  92.9 0.1 copy.99
  93.0 1.0 and_and_fusion
  94.1 0.1 copy.78
  94.2 0.1 copy.80
  94.3 5.3 %collective-permute-done = bf16[256,2,128]{0,2,1:T(8,128)(2,1)S(1)} collective-permute-done((bf16[256,2,128]{0,2,1:T(8,128)(2,1)S(1)}, bf16[256,2,128]{0,2,1:T(8,128)(2,1)S(1)}, u32[]{:S(2)}, u32[]{:S(2)}) %collective-permute-start) | collective-permute-done | bytes 131104 | tf_op jit(solution)/shard_map/ppermute | solution.py:19
  99.6 5.4 %collective-permute-start.5 = (bf16[256,2,128]{2,0,1:T(8,128)(2,1)S(1)}, bf16[256,2,128]{2,0,1:T(8,128)(2,1)S(1)}, u32[]{:S(2)}, u32[]{:S(2)}) collective-permute-start(bf16[256,2,128]{2,0,1:T(8,128)(2,1)S(1)} %copy.66), channel_id=1, source_target_pairs={{0,24},{8,32},{16,40},{24,48},{32,56},{40,64},{48,72},{56,80},{64,... | collective-permute-start | bytes 393224 | tf_op jit(solution)/shard_map/ppermute | solution.py:19
  105.0 0.0 collective-permute-done.1
  105.0 5.0 %collective-permute-start.6 = (bf16[256,2,128]{2,0,1:T(8,128)(2,1)S(1)}, bf16[256,2,128]{2,0,1:T(8,128)(2,1)S(1)}, u32[]{:S(2)}, u32[]{:S(2)}) collective-permute-start(bf16[256,2,128]{2,0,1:T(8,128)(2,1)S(1)} %copy.66), channel_id=1, source_target_pairs={{0,16},{8,24},{16,32},{24,40},{32,48},{40,56},{48,64},{56,72},{64,... | collective-permute-start | bytes 393224 | tf_op jit(solution)/shard_map/ppermute | solution.py:19
  110.1 3.0 %collective-permute-start.7 = (bf16[256,2,128]{2,0,1:T(8,128)(2,1)S(1)}, bf16[256,2,128]{2,0,1:T(8,128)(2,1)S(1)}, u32[]{:S(2)}, u32[]{:S(2)}) collective-permute-start(bf16[256,2,128]{2,0,1:T(8,128)(2,1)S(1)} %copy.66), channel_id=1, source_target_pairs={{0,8},{8,16},{16,24},{24,32},{32,40},{40,48},{48,56},{56,64},{64,7... | collective-permute-start | bytes 393224 | tf_op jit(solution)/shard_map/ppermute | solution.py:19
  113.0 0.0 collective-permute-done.3
  113.1 0.2 copy.83
  113.3 0.0 all-to-all-done.2
  113.3 0.4 slice_bitcast_fusion.1
  113.7 0.2 copy.89
  113.8 0.2 copy.88
  114.0 0.5 fusion.9
  114.5 0.1 fusion.40
  114.7 0.3 convolution_convert_fusion
  115.0 0.9 copy.110
  115.9 13.7 %all-to-all-start.3 = ((bf16[64,2,4,2,128]{4,3,2,1,0:T(2,128)(2,1)}), bf16[64,2,4,2,128]{4,3,2,1,0:T(2,128)(2,1)S(1)}, u32[]{:S(2)}, u32[]{:S(2)}) async-start(bf16[64,2,4,2,128]{4,3,2,1,0:T(2,128)(2,1)} %bitcast.89), calls=%async_computation.3 | async-start | bytes 524288 | tf_op jit(solution)/shard_map/all_to_all | solution.py:143
  129.6 0.0 collective-permute-done.4
  129.8 1.0 fusion.41
  130.8 1.3 fusion.10
  132.1 0.1 copy.93
  132.2 18.8 %all-to-all-done.3 = bf16[64,2,4,2,128]{4,3,2,1,0:T(2,128)(2,1)S(1)} async-done(((bf16[64,2,4,2,128]{4,3,2,1,0:T(2,128)(2,1)}), bf16[64,2,4,2,128]{4,3,2,1,0:T(2,128)(2,1)S(1)}, u32[]{:S(2)}, u32[]{:S(2)}) %all-to-all-start.3) | async-done | bytes 262176 | tf_op jit(solution)/shard_map/all_to_all | solution.py:143
  151.1 1.3 gather_fusion
  152.4 0.7 pad_maximum_fusion
  (37 shorter events, 0.5 us)
Async XLA Ops:
  2.2 0.7 copy-start.3
  2.3 23.7 %copy-start = (bf16[256,512]{1,0:T(8,128)(2,1)S(1)}, bf16[256,512]{1,0:T(8,128)(2,1)}, u32[]{:S(2)}) copy-start(bf16[256,512]{1,0:T(8,128)(2,1)} %param.4) | copy-start | bytes 786436
  7.2 36.4 %all-to-all-start = ((s32[64,2,4,2]{2,3,1,0:T(2,128)}), s32[64,2,4,2]{2,3,1,0:T(2,128)S(1)}, u32[]{:S(2)}, u32[]{:S(2)}) async-start(s32[64,2,4,2]{2,3,1,0:T(2,128)} %copy.76), calls=%async_computation | async-start | bytes 262144 | tf_op jit(solution)/shard_map/all_to_all | solution.py:135
  26.0 22.3 %copy-start.1 = (bf16[256,512]{1,0:T(8,128)(2,1)S(1)}, bf16[256,512]{1,0:T(8,128)(2,1)}, u32[]{:S(2)}) copy-start(bf16[256,512]{1,0:T(8,128)(2,1)} %param.6) | copy-start | bytes 786436
  43.6 26.3 %all-to-all-start.1 = ((bf16[64,2,4,2,128]{4,3,2,1,0:T(2,128)(2,1)}), bf16[64,2,4,2,128]{4,3,2,1,0:T(2,128)(2,1)S(1)}, u32[]{:S(2)}, u32[]{:S(2)}) async-start(bf16[64,2,4,2,128]{4,3,2,1,0:T(2,128)(2,1)} %bitcast.17), calls=%async_computation.1 | async-start | bytes 524288 | tf_op jit(solution)/shard_map/all_to_all | solution.py:137
  48.2 1.0 copy-start.2
  69.9 43.3 %all-to-all-start.2 = ((bf16[64,2,4,2,256]{4,3,2,1,0:T(2,128)(2,1)}), bf16[64,2,4,2,256]{4,3,2,1,0:T(2,128)(2,1)S(1)}, u32[]{:S(2)}, u32[]{:S(2)}) async-start(bf16[64,2,4,2,256]{4,3,2,1,0:T(2,128)(2,1)} %reshape.336), calls=%async_computation.2 | async-start | bytes 1048576 | tf_op jit(solution)/shard_map/all_to_all | solution.py:128
  74.8 24.8 %collective-permute-start = (bf16[256,2,128]{0,2,1:T(8,128)(2,1)S(1)}, bf16[256,2,128]{0,2,1:T(8,128)(2,1)S(1)}, u32[]{:S(2)}, u32[]{:S(2)}) collective-permute-start(bf16[256,2,128]{0,2,1:T(8,128)(2,1)S(1)} %bitcast.98), channel_id=1, source_target_pairs={{0,32},{8,40},{16,48},{24,56},{32,64},{40,72},{48,80},{56,88},{64,... | collective-permute-start | bytes 393224 | tf_op jit(solution)/shard_map/ppermute | solution.py:19
  78.2 26.8 %collective-permute-start.1 = (bf16[256,2,128]{0,2,1:T(8,128)(2,1)S(1)}, bf16[256,2,128]{0,2,1:T(8,128)(2,1)S(1)}, u32[]{:S(2)}, u32[]{:S(2)}) collective-permute-start(bf16[256,2,128]{0,2,1:T(8,128)(2,1)S(1)} %bitcast.99), channel_id=1, source_target_pairs={{0,24},{8,32},{16,40},{24,48},{32,56},{40,64},{48,72},{56,80},{64,... | collective-permute-start | bytes 393224 | tf_op jit(solution)/shard_map/ppermute | solution.py:19
  82.8 27.2 %collective-permute-start.2 = (bf16[256,2,128]{0,2,1:T(8,128)(2,1)S(1)}, bf16[256,2,128]{0,2,1:T(8,128)(2,1)S(1)}, u32[]{:S(2)}, u32[]{:S(2)}) collective-permute-start(bf16[256,2,128]{0,2,1:T(8,128)(2,1)S(1)} %bitcast.100), channel_id=1, source_target_pairs={{0,16},{8,24},{16,32},{24,40},{32,48},{40,56},{48,64},{56,72},{64,... | collective-permute-start | bytes 393224 | tf_op jit(solution)/shard_map/ppermute | solution.py:19
  86.5 26.5 %collective-permute-start.3 = (bf16[256,2,128]{0,2,1:T(8,128)(2,1)S(1)}, bf16[256,2,128]{0,2,1:T(8,128)(2,1)S(1)}, u32[]{:S(2)}, u32[]{:S(2)}) collective-permute-start(bf16[256,2,128]{0,2,1:T(8,128)(2,1)S(1)} %bitcast.101), channel_id=1, source_target_pairs={{0,8},{8,16},{16,24},{24,32},{32,40},{40,48},{48,56},{56,64},{64,7... | collective-permute-start | bytes 393224 | tf_op jit(solution)/shard_map/ppermute | solution.py:19
  89.5 40.1 %collective-permute-start.4 = (bf16[256,2,128]{2,0,1:T(8,128)(2,1)S(1)}, bf16[256,2,128]{2,0,1:T(8,128)(2,1)S(1)}, u32[]{:S(2)}, u32[]{:S(2)}) collective-permute-start(bf16[256,2,128]{2,0,1:T(8,128)(2,1)S(1)} %copy.66), channel_id=1, source_target_pairs={{0,32},{8,40},{16,48},{24,56},{32,64},{40,72},{48,80},{56,88},{64,... | collective-permute-start | bytes 393224 | tf_op jit(solution)/shard_map/ppermute | solution.py:19
  99.6 30.1 %collective-permute-start.5 = (bf16[256,2,128]{2,0,1:T(8,128)(2,1)S(1)}, bf16[256,2,128]{2,0,1:T(8,128)(2,1)S(1)}, u32[]{:S(2)}, u32[]{:S(2)}) collective-permute-start(bf16[256,2,128]{2,0,1:T(8,128)(2,1)S(1)} %copy.66), channel_id=1, source_target_pairs={{0,24},{8,32},{16,40},{24,48},{32,56},{40,64},{48,72},{56,80},{64,... | collective-permute-start | bytes 393224 | tf_op jit(solution)/shard_map/ppermute | solution.py:19
  105.0 24.7 %collective-permute-start.6 = (bf16[256,2,128]{2,0,1:T(8,128)(2,1)S(1)}, bf16[256,2,128]{2,0,1:T(8,128)(2,1)S(1)}, u32[]{:S(2)}, u32[]{:S(2)}) collective-permute-start(bf16[256,2,128]{2,0,1:T(8,128)(2,1)S(1)} %copy.66), channel_id=1, source_target_pairs={{0,16},{8,24},{16,32},{24,40},{32,48},{40,56},{48,64},{56,72},{64,... | collective-permute-start | bytes 393224 | tf_op jit(solution)/shard_map/ppermute | solution.py:19
  110.1 19.7 %collective-permute-start.7 = (bf16[256,2,128]{2,0,1:T(8,128)(2,1)S(1)}, bf16[256,2,128]{2,0,1:T(8,128)(2,1)S(1)}, u32[]{:S(2)}, u32[]{:S(2)}) collective-permute-start(bf16[256,2,128]{2,0,1:T(8,128)(2,1)S(1)} %copy.66), channel_id=1, source_target_pairs={{0,8},{8,16},{16,24},{24,32},{32,40},{40,48},{48,56},{56,64},{64,7... | collective-permute-start | bytes 393224 | tf_op jit(solution)/shard_map/ppermute | solution.py:19
  115.9 35.2 %all-to-all-start.3 = ((bf16[64,2,4,2,128]{4,3,2,1,0:T(2,128)(2,1)}), bf16[64,2,4,2,128]{4,3,2,1,0:T(2,128)(2,1)S(1)}, u32[]{:S(2)}, u32[]{:S(2)}) async-start(bf16[64,2,4,2,128]{4,3,2,1,0:T(2,128)(2,1)} %bitcast.89), calls=%async_computation.3 | async-start | bytes 524288 | tf_op jit(solution)/shard_map/all_to_all | solution.py:143
where the time goes:
time: 154 us; the launch traced here: 153 us
  starting transfers between devices  73 us (47%)
  waiting for transfers between devices  56.2 us (36%)
  local copies, waits for them, and re-layouts  15 us (10%)
  other arithmetic  5.3 us (3%)
  matrix products  3.11 us (2%)
    ppermute x8, starting transfers between devices, shifted(): lax.ppermute(value, axis, [(source, source + steps) for source in range(i...  31.2 us
    all_to_all x1, waiting for transfers between devices, per_device(): lax.all_to_all(mixed, 'seq', split_axis=0, concat_axis=0, tiled=True)  18.8 us
    all_to_all x1, starting transfers between devices, per_device(): lax.all_to_all(send_pos, 'seq', split_axis=0, concat_axis=0, tiled=True)  18.7 us
    all_to_all x1, waiting for transfers between devices, per_device(): lax.all_to_all(packed([heads_first(query_rows)]), 'seq', split_axis=0, co...  17 us
    all_to_all x1, waiting for transfers between devices, per_device(): lax.all_to_all(send_pos, 'seq', split_axis=0, concat_axis=0, tiled=True)  15 us
    all_to_all x1, starting transfers between devices, per_device(): lax.all_to_all(mixed, 'seq', split_axis=0, concat_axis=0, tiled=True)  13.7 us
    ppermute x8, waiting for transfers between devices, shifted(): lax.ppermute(value, axis, [(source, source + steps) for source in range(i...  5.35 us
    all_to_all x1, starting transfers between devices, per_device(): lax.all_to_all(packed([heads_first(key_rows), heads_first(value_rows)]),...  4.7 us
  transfers between devices with their start and end apart: 12, of which 4 were waited for; matrix products, arithmetic and copies ran while one was open for 9% of the time, Pallas kernels for 0%

commit v1 on v0

v1 whole, which is shorter than its diff:
```python
import math

import jax
import jax.numpy as jnp
from jax import lax
from jax.experimental import pallas as pl
from jax.experimental.pallas import tpu as pltpu
from jax.sharding import PartitionSpec as P

CLUSTERS = 256
SRC_CAP = 2
SEQ = 64
ROWS_Z = 16
ROWS_Y = 4
TOK = 256
HD = 128
PAIR = 2
SPLIT = PAIR * HD
OWNED = CLUSTERS // SEQ
ROOM = OWNED * SRC_CAP
SLOTS = SEQ * ROOM
SPAN = 4
MASKED = -1e30
EMPTY = 2.0**60
EMPTY_TEST = 2.0**50
NT = (((1,), (1,)), ((), ()))


def dot(a, b, dims=(((1,), (0,)), ((), ()))):
    return lax.dot_general(a, b, dims, preferred_element_type=jnp.float32)


def blend(scores, value_block):
    largest = jnp.max(scores, axis=-1, keepdims=True)
    raised = jnp.exp(scores - largest)
    weights = (raised * (1.0 / jnp.sum(raised, axis=-1, keepdims=True))).astype(jnp.bfloat16)
    return dot(weights, value_block)


def kernel(q_ref, k_ref, v_ref, idc_ref, idr_ref, out_ref,
           send, recv, osend, home, win,
           own_sem, send_sem, recv_sem, osend_sem, home_sem, win_send, win_recv):
    me = lax.axis_index("seq")
    z, y = me // ROWS_Y, me % ROWS_Y
    scale = 1.0 / math.sqrt(HD)

    def each_peer(act):
        def step(i, carry):
            m = (i + 1) // 2
            dz = (8 - m) * (2 * (i % 2) - 1)
            pz = (z + dz + ROWS_Z) % ROWS_Z
            for dy in range(ROWS_Y):
                act(pz * ROWS_Y + (y + dy) % ROWS_Y)
            return carry

        lax.fori_loop(0, ROWS_Z - 1, step, 0)
        for dy in range(1, ROWS_Y):
            act(z * ROWS_Y + (y + dy) % ROWS_Y)

    barrier = pltpu.get_barrier_semaphore()
    each_peer(lambda peer: pl.semaphore_signal(barrier, inc=1, device_id={"seq": peer}))

    own_k = pltpu.make_async_copy(k_ref.at[:, pl.ds(0, SPLIT)], win.at[0, :, pl.ds(0, SPLIT)], own_sem.at[0])
    own_v = pltpu.make_async_copy(v_ref.at[:, pl.ds(0, SPLIT)], win.at[0, :, pl.ds(SPLIT, SPLIT)], own_sem.at[1])
    own_k.start()
    own_v.start()

    earlier = lax.broadcasted_iota(jnp.int32, (TOK, TOK), 0) < lax.broadcasted_iota(jnp.int32, (TOK, TOK), 1)
    later = lax.broadcasted_iota(jnp.int32, (TOK, TOK), 0) > lax.broadcasted_iota(jnp.int32, (TOK, TOK), 1)
    slot_cols = []
    for h in range(PAIR):
        id_col = idc_ref[h]
        id_row = idr_ref[h:h + 1, :]
        same = id_col == id_row
        rank_row = jnp.sum(jnp.where(same & earlier, 1, 0), axis=0, keepdims=True)
        rank_col = jnp.sum(jnp.where(same & later, 1, 0), axis=1, keepdims=True)
        slot_row = id_row * SRC_CAP + rank_row
        slot_cols.append(id_col * SRC_CAP + rank_col)
        pick = jnp.where(lax.broadcasted_iota(jnp.int32, (SLOTS, TOK), 0) == slot_row, 1.0, 0.0)
        blank = (1.0 - jnp.sum(pick, axis=1, keepdims=True)) * EMPTY
        pick = pick.astype(jnp.bfloat16)
        cols = pl.ds(SPLIT + h * HD, HD)
        packed_q = dot(pick, q_ref[:, cols])
        packed_k = dot(pick, k_ref[:, cols])
        packed_v = dot(pick, v_ref[:, cols]) + blank
        for n, packed in enumerate((packed_q, packed_k, packed_v)):
            send[h, :, :, n * HD:(n + 1) * HD] = packed.reshape(SEQ, ROOM, HD).astype(jnp.bfloat16)

    own_k.wait()
    own_v.wait()
    pl.semaphore_wait(barrier, SEQ - 1)

    def push(source, target, from_sem, to_sem):
        def act(peer):
            pltpu.make_async_remote_copy(
                src_ref=source.at[peer], dst_ref=target.at[me],
                send_sem=from_sem, recv_sem=to_sem, device_id={"seq": peer},
            ).start()
        return act

    def arrived(buffer, from_sem, to_sem):
        return pltpu.make_async_remote_copy(
            src_ref=buffer.at[pl.ds(0, SEQ - 1)], dst_ref=buffer.at[pl.ds(0, SEQ - 1)],
            send_sem=from_sem, recv_sem=to_sem, device_id={"seq": (me + 1) % SEQ},
        )

    def own_chunk(source, target, sem):
        return pltpu.make_async_copy(source.at[me], target.at[me], sem)

    for h in range(PAIR):
        each_peer(push(send.at[h], recv.at[h], send_sem.at[h], recv_sem.at[h]))
        own_chunk(send.at[h], recv.at[h], own_sem.at[2 + h]).start()

    def window(src_slot, dst_slot, peer):
        return pltpu.make_async_remote_copy(
            src_ref=win.at[src_slot], dst_ref=win.at[dst_slot],
            send_sem=win_send.at[dst_slot - 1], recv_sem=win_recv.at[dst_slot - 1],
            device_id={"seq": peer},
        )

    ahead = window(0, SPAN, (me + ROWS_Y) % SEQ)
    ahead.start()

    def sideways(dy):
        return window(SPAN * ((y + dy) // ROWS_Y), dy, z * ROWS_Y + (y + dy) % ROWS_Y)

    for dy in range(1, ROWS_Y):
        @pl.when(y + dy < ROWS_Y)
        def _(dy=dy):
            sideways(dy).start()

    def routed(h):
        arrived(recv.at[h], send_sem.at[h], recv_sem.at[h]).wait_recv()
        own_chunk(send.at[h], recv.at[h], own_sem.at[2 + h]).wait()
        q, k, v = (
            recv[h, :, :, n * HD:(n + 1) * HD].astype(jnp.float32).reshape(SLOTS, HD).astype(jnp.bfloat16)
            for n in range(3)
        )
        probe = jnp.where(lax.broadcasted_iota(jnp.int32, (16, HD), 1) == 0, 1.0, 0.0).astype(jnp.bfloat16)
        first = dot(probe, v, NT)[0:1, :]
        absent = jnp.where(first > EMPTY_TEST, MASKED, 0.0)
        block = 128
        for b in range(SLOTS // block):
            lo, hi = b * block, (b + 1) * block
            row = lax.broadcasted_iota(jnp.int32, (block, hi), 0) + lo
            col = lax.broadcasted_iota(jnp.int32, (block, hi), 1)
            allowed = (col <= row) & ((row & (ROOM - SRC_CAP)) == (col & (ROOM - SRC_CAP)))
            scores = dot(q[lo:hi], k[:hi], NT) * scale + absent[:, :hi]
            mixed = blend(jnp.where(allowed, scores, MASKED), v[:hi])
            osend[h, b * 16:(b + 1) * 16] = mixed.reshape(16, ROOM, HD).astype(jnp.bfloat16)
        each_peer(push(osend.at[h], home.at[h], osend_sem.at[h], home_sem.at[h]))
        own_chunk(osend.at[h], home.at[h], own_sem.at[4 + h]).start()

    routed(0)
    ahead.wait_recv()
    for dy in range(1, ROWS_Y):
        @pl.when(y + dy >= ROWS_Y)
        def _(dy=dy):
            sideways(dy).start()
    routed(1)

    for dy in range(1, ROWS_Y):
        sideways(dy).wait_recv()
    width = (SPAN + 1) * TOK
    row = lax.broadcasted_iota(jnp.int32, (TOK, width), 0)
    col = lax.broadcasted_iota(jnp.int32, (TOK, width), 1)
    slot, at = col // TOK, col % TOK
    gap = row - at + slot * TOK
    allowed = (gap >= 0) & (gap < SPAN * TOK) & (slot <= me)
    for h in range(PAIR):
        k = win[:, :, h * HD:(h + 1) * HD].reshape(width, HD)
        v = win[:, :, SPLIT + h * HD:SPLIT + (h + 1) * HD].reshape(width, HD)
        scores = dot(q_ref[:, h * HD:(h + 1) * HD], k, NT) * scale
        mixed = blend(jnp.where(allowed, scores, MASKED), v)
        out_ref[:, h * HD:(h + 1) * HD] = mixed.astype(jnp.bfloat16)

    for h in range(PAIR):
        back = jnp.where(lax.broadcasted_iota(jnp.int32, (TOK, SLOTS), 1) == slot_cols[h], 1.0, 0.0).astype(jnp.bfloat16)
        arrived(home.at[h], osend_sem.at[h], home_sem.at[h]).wait_recv()
        own_chunk(osend.at[h], home.at[h], own_sem.at[4 + h]).wait()
        rows = home[h].astype(jnp.float32).reshape(SLOTS, HD).astype(jnp.bfloat16)
        out_ref[:, SPLIT + h * HD:SPLIT + (h + 1) * HD] = dot(back, rows).astype(jnp.bfloat16)

    for h in range(PAIR):
        arrived(recv.at[h], send_sem.at[h], recv_sem.at[h]).wait_send()
        arrived(home.at[h], osend_sem.at[h], home_sem.at[h]).wait_send()
    ahead.wait_send()
    for dy in range(1, ROWS_Y):
        sideways(dy).wait_send()


def per_device(query_rows, key_rows, value_rows, cluster_ids):
    vmem = pl.BlockSpec(memory_space=pltpu.VMEM)
    return pl.pallas_call(
        kernel,
        out_shape=jax.ShapeDtypeStruct(query_rows.shape, jnp.bfloat16),
        in_specs=[vmem] * 5,
        out_specs=vmem,
        scratch_shapes=[
            pltpu.VMEM((PAIR, SEQ, ROOM, 3 * HD), jnp.bfloat16),
            pltpu.VMEM((PAIR, SEQ, ROOM, 3 * HD), jnp.bfloat16),
            pltpu.VMEM((PAIR, SEQ, ROOM, HD), jnp.bfloat16),
            pltpu.VMEM((PAIR, SEQ, ROOM, HD), jnp.bfloat16),
            pltpu.VMEM((SPAN + 1, TOK, 2 * SPLIT), jnp.bfloat16),
            pltpu.SemaphoreType.DMA((6,)),
            pltpu.SemaphoreType.DMA((PAIR,)),
            pltpu.SemaphoreType.DMA((PAIR,)),
            pltpu.SemaphoreType.DMA((PAIR,)),
            pltpu.SemaphoreType.DMA((PAIR,)),
            pltpu.SemaphoreType.DMA((SPAN,)),
            pltpu.SemaphoreType.DMA((SPAN,)),
        ],
        compiler_params=pltpu.CompilerParams(
            collective_id=0, has_side_effects=True, vmem_limit_bytes=48 * 1024 * 1024
        ),
    )(query_rows, key_rows, value_rows, cluster_ids, cluster_ids[:, :, 0])


def solution(mesh):
    in_specs = (P("seq", "head"), P("seq", "head"), P("seq", "head"), P("head", "seq", None))
    out_specs = P("seq", "head")
    return jax.shard_map(
        per_device, mesh=mesh, in_specs=in_specs, out_specs=out_specs, check_vma=False
    )
```

time: 154 us -> 80 us (0.52)
  Pallas kernels: 0 us -> 75.3 us
  starting transfers between devices: 73 us -> 0 us
  waiting for transfers between devices: 56.2 us -> 0 us
  local copies, waits for them, and re-layouts: 15 us -> 3.58 us
  other arithmetic: 5.3 us -> 0 us
  matrix products: 3.11 us -> 0 us
    pallas_call x0 -> x1, Pallas kernels: none -> 75.3 us  [per_device(): pl.pallas_call(kernel, out_shape=jax.ShapeDtypeStruct(query_rows.shape, j...]
    all_to_all x4 -> x0, waiting for transfers between devices: 50.8 us -> none  [the longest x1 18.8 us: per_device(): lax.all_to_all(mixed, 'seq', split_axis=0, concat_axis=0, tiled=True)]
    all_to_all x4 -> x0, starting transfers between devices: 41.8 us -> none  [the longest x1 18.7 us: per_device(): lax.all_to_all(send_pos, 'seq', split_axis=0, concat_axis=0, tiled=True)]
    ppermute x8 -> x0, starting transfers between devices: 31.2 us -> none  [shifted(): lax.ppermute(value, axis, [(source, source + steps) for source in range(i...]
    ppermute x8 -> x0, waiting for transfers between devices: 5.35 us -> none  [shifted(): lax.ppermute(value, axis, [(source, source + steps) for source in range(i...]
    scatter x2 -> x0, local copies, waits for them, and re-layouts: 4.88 us -> none  [the longest x1 2.45 us: per_device(): send_pos = jnp.full((seq_count * per_dest,), -1, jnp.int32).at[target].se...]
    reshape x7 -> x0, local copies, waits for them, and re-layouts: 3.92 us -> none  [the longest x2 1.8 us: per_device(): send_pos = jnp.full((seq_count * per_dest,), -1, jnp.int32).at[target].se...]
    scatter x1 -> x0, other arithmetic: 2.49 us -> none  [packed(): jnp.zeros((seq_count * per_dest, span_cols), jnp.bfloat16).at[target]]
  transfers between devices with their start and end apart: 12 -> 0, of which waited for: 4 -> 0; matrix products, arithmetic and copies ran while one was open for 9% -> 0% of each run, Pallas kernels for 0% -> 0%
where the time goes in v1:
time: 80 us; the launch traced here: 78.9 us
  Pallas kernels  75.3 us (94%)
  local copies, waits for them, and re-layouts  3.58 us (4%)
    pallas_call x1, Pallas kernels, per_device(): pl.pallas_call(kernel, out_shape=jax.ShapeDtypeStruct(query_rows.shape, j...  75.3 us
    unnamed x11, local copies, waits for them, and re-layouts  3.58 us

profile of v1, /device:TPU:6, one launch (start us, length us, event | category | flops | bytes accessed | tf_op | source)
XLA Modules:
  0.0 78.9 jit_solution(18280842285216968834)
XLA Ops:
  0.0 0.0 copy-start.3
  0.0 0.0 copy-start
  0.0 0.8 copy.8
  0.8 0.0 copy-done.3
  0.8 0.1 copy.5.idc_ref
  0.9 0.1 copy-done
  1.0 0.0 copy-start.1
  1.0 0.9 %copy-done.1 = bf16[256,512]{1,0:T(8,128)(2,1)S(1)} copy-done((bf16[256,512]{1,0:T(8,128)(2,1)S(1)}, bf16[256,512]{1,0:T(8,128)(2,1)}, u32[]{:S(2)}) %copy-start.1) | copy-done | bytes 262168
  1.9 0.0 copy-start.2
  1.9 0.9 %copy-done.2 = bf16[256,512]{1,0:T(8,128)(2,1)S(1)} copy-done((bf16[256,512]{1,0:T(8,128)(2,1)S(1)}, bf16[256,512]{1,0:T(8,128)(2,1)}, u32[]{:S(2)}) %copy-start.2) | copy-done | bytes 262168
  2.9 75.3 %shard_map.46 = bf16[256,512]{1,0:T(8,128)(2,1)S(1)} custom-call(bf16[256,512]{1,0:T(8,128)(2,1)S(1)} %copy-done, bf16[256,512]{1,0:T(8,128)(2,1)S(1)} %copy-done.1, bf16[256,512]{1,0:T(8,128)(2,1)S(1)} %copy-done.2, s32[2,256,1]{2,1,0:T(8,128)S(1)} %copy.5.idc_ref, s32[2,256]{1,0:T(2,128)S(1)} %bitcast.3), custom_call_target="tpu_custom_call" | custom-call | tf_op jit(solution)/shard_map/pallas_call | solution.py:194
  78.2 0.7 copy.10
Async XLA Ops:
  0.0 0.8 copy-start.3
  0.0 1.0 %copy-start = (bf16[256,512]{1,0:T(8,128)(2,1)S(1)}, bf16[256,512]{1,0:T(8,128)(2,1)}, u32[]{:S(2)}) copy-start(bf16[256,512]{1,0:T(8,128)(2,1)} %q_ref.1) | copy-start | bytes 786436
  1.0 0.9 %copy-start.1 = (bf16[256,512]{1,0:T(8,128)(2,1)S(1)}, bf16[256,512]{1,0:T(8,128)(2,1)}, u32[]{:S(2)}) copy-start(bf16[256,512]{1,0:T(8,128)(2,1)} %k_ref.1) | copy-start | bytes 786436
  1.9 0.9 %copy-start.2 = (bf16[256,512]{1,0:T(8,128)(2,1)S(1)}, bf16[256,512]{1,0:T(8,128)(2,1)}, u32[]{:S(2)}) copy-start(bf16[256,512]{1,0:T(8,128)(2,1)} %v_ref.1) | copy-start | bytes 786436

commit v2 on v1

--- a/solution.py
+++ b/solution.py
@@ -37,40 +37,81 @@
     return dot(weights, value_block)
 
 
-def kernel(q_ref, k_ref, v_ref, idc_ref, idr_ref, out_ref,
-           send, recv, osend, home, win,
-           own_sem, send_sem, recv_sem, osend_sem, home_sem, win_send, win_recv):
+def kernel(q_hbm, k_hbm, v_hbm, id_hbm, out_ref,
+           q_ref, k_ref, v_ref, id_ref, send, recv, osend, home, win, stop,
+           load_sem, own_sem, send_sem, recv_sem, osend_sem, home_sem, win_send, win_recv, ready,
+           leg_send, leg_recv, hop_send):
     me = lax.axis_index("seq")
     z, y = me // ROWS_Y, me % ROWS_Y
     scale = 1.0 / math.sqrt(HD)
 
-    def each_peer(act):
+    def at_distance(dz, act, away=True):
+        for dy in range(ROWS_Y):
+            if away or dy:
+                act((z + dz + ROWS_Z) % ROWS_Z * ROWS_Y + (y + dy) % ROWS_Y)
+
+    def each_peer(act, nearer=0):
         def step(i, carry):
             m = (i + 1) // 2
-            dz = (8 - m) * (2 * (i % 2) - 1)
-            pz = (z + dz + ROWS_Z) % ROWS_Z
-            for dy in range(ROWS_Y):
-                act(pz * ROWS_Y + (y + dy) % ROWS_Y)
+            at_distance((8 - m) * (2 * (i % 2) - 1), act)
             return carry
 
-        lax.fori_loop(0, ROWS_Z - 1, step, 0)
-        for dy in range(1, ROWS_Y):
-            act(z * ROWS_Y + (y + dy) % ROWS_Y)
+        lax.fori_loop(nearer, ROWS_Z - 1, step, 0)
+        at_distance(0, act, False)
 
     barrier = pltpu.get_barrier_semaphore()
-    each_peer(lambda peer: pl.semaphore_signal(barrier, inc=1, device_id={"seq": peer}))
-
-    own_k = pltpu.make_async_copy(k_ref.at[:, pl.ds(0, SPLIT)], win.at[0, :, pl.ds(0, SPLIT)], own_sem.at[0])
-    own_v = pltpu.make_async_copy(v_ref.at[:, pl.ds(0, SPLIT)], win.at[0, :, pl.ds(SPLIT, SPLIT)], own_sem.at[1])
-    own_k.start()
-    own_v.start()
+
+    def greet(peer):
+        pl.semaphore_signal(barrier, inc=1, device_id={"seq": peer})
+
+    for dz in (1, -1, 0):
+        at_distance(dz, greet, dz != 0)
+
+    def widen(n):
+        for dz in (1 << n, -(1 << n)):
+            peer = (z + dz + ROWS_Z) % ROWS_Z * ROWS_Y + y
+            pl.semaphore_signal(ready.at[n], inc=1, device_id={"seq": peer})
+
+    loads = [
+        pltpu.make_async_copy(source, target, load_sem.at[n])
+        for n, (source, target) in enumerate(
+            ((id_hbm, id_ref), (q_hbm, q_ref), (k_hbm, k_ref), (v_hbm, v_ref),
+             (k_hbm.at[:, pl.ds(0, SPLIT)], win.at[0, :, pl.ds(0, SPLIT)]),
+             (v_hbm.at[:, pl.ds(0, SPLIT)], win.at[0, :, pl.ds(SPLIT, SPLIT)]))
+        )
+    ]
+    for load in loads:
+        load.start()
+
+    def window(src_slot, dst_slot, peer):
+        return pltpu.make_async_remote_copy(
+            src_ref=win.at[src_slot], dst_ref=win.at[dst_slot],
+            send_sem=win_send.at[dst_slot - 1], recv_sem=win_recv.at[dst_slot - 1],
+            device_id={"seq": peer},
+        )
+
+    ahead = window(0, SPAN, (me + ROWS_Y) % SEQ)
+
+    def sideways(dy):
+        return window(SPAN * ((y + dy) // ROWS_Y), dy, z * ROWS_Y + (y + dy) % ROWS_Y)
+
+    pl.semaphore_wait(barrier, 3 * ROWS_Y - 1)
+    widen(0)
+    for load in loads:
+        load.wait()
+    ahead.start()
+    for dy in range(1, ROWS_Y):
+        @pl.when(y + dy < ROWS_Y)
+        def _(dy=dy):
+            sideways(dy).start()
 
     earlier = lax.broadcasted_iota(jnp.int32, (TOK, TOK), 0) < lax.broadcasted_iota(jnp.int32, (TOK, TOK), 1)
     later = lax.broadcasted_iota(jnp.int32, (TOK, TOK), 0) > lax.broadcasted_iota(jnp.int32, (TOK, TOK), 1)
+    diagonal = ~(earlier | later)
     slot_cols = []
     for h in range(PAIR):
-        id_col = idc_ref[h]
-        id_row = idr_ref[h:h + 1, :]
+        id_row = id_ref[h]
+        id_col = jnp.sum(jnp.where(diagonal, id_row, 0), axis=1, keepdims=True)
         same = id_col == id_row
         rank_row = jnp.sum(jnp.where(same & earlier, 1, 0), axis=0, keepdims=True)
         rank_col = jnp.sum(jnp.where(same & later, 1, 0), axis=1, keepdims=True)
@@ -86,10 +127,6 @@
         for n, packed in enumerate((packed_q, packed_k, packed_v)):
             send[h, :, :, n * HD:(n + 1) * HD] = packed.reshape(SEQ, ROOM, HD).astype(jnp.bfloat16)
 
-    own_k.wait()
-    own_v.wait()
-    pl.semaphore_wait(barrier, SEQ - 1)
-
     def push(source, target, from_sem, to_sem):
         def act(peer):
             pltpu.make_async_remote_copy(
@@ -98,6 +135,27 @@
             ).start()
         return act
 
+    def leg(h, dy):
+        to_y = (y + dy) % ROWS_Y
+        return pltpu.make_async_remote_copy(
+            src_ref=send.at[h, (z + 8) % ROWS_Z * ROWS_Y + to_y], dst_ref=stop.at[h, y],
+            send_sem=leg_send.at[h], recv_sem=leg_recv.at[h],
+            device_id={"seq": (z + 12) % ROWS_Z * ROWS_Y + to_y},
+        )
+
+    def legs(h):
+        return pltpu.make_async_remote_copy(
+            src_ref=stop.at[h], dst_ref=stop.at[h], send_sem=leg_send.at[h], recv_sem=leg_recv.at[h],
+            device_id={"seq": (me + 1) % SEQ},
+        )
+
+    def onward(h):
+        return pltpu.make_async_remote_copy(
+            src_ref=stop.at[h], dst_ref=recv.at[h, pl.ds((z + 4) % ROWS_Z * ROWS_Y, ROWS_Y)],
+            send_sem=hop_send.at[h], recv_sem=recv_sem.at[h],
+            device_id={"seq": (z + 12) % ROWS_Z * ROWS_Y + y},
+        )
+
     def arrived(buffer, from_sem, to_sem):
         return pltpu.make_async_remote_copy(
             src_ref=buffer.at[pl.ds(0, SEQ - 1)], dst_ref=buffer.at[pl.ds(0, SEQ - 1)],
@@ -107,31 +165,38 @@
     def own_chunk(source, target, sem):
         return pltpu.make_async_copy(source.at[me], target.at[me], sem)
 
-    for h in range(PAIR):
-        each_peer(push(send.at[h], recv.at[h], send_sem.at[h], recv_sem.at[h]))
-        own_chunk(send.at[h], recv.at[h], own_sem.at[2 + h]).start()
-
-    def window(src_slot, dst_slot, peer):
-        return pltpu.make_async_remote_copy(
-            src_ref=win.at[src_slot], dst_ref=win.at[dst_slot],
-            send_sem=win_send.at[dst_slot - 1], recv_sem=win_recv.at[dst_slot - 1],
-            device_id={"seq": peer},
-        )
-
-    ahead = window(0, SPAN, (me + ROWS_Y) % SEQ)
-    ahead.start()
-
-    def sideways(dy):
-        return window(SPAN * ((y + dy) // ROWS_Y), dy, z * ROWS_Y + (y + dy) % ROWS_Y)
-
+    first_push = push(send.at[0], recv.at[0], send_sem.at[0], recv_sem.at[0])
+    for dz in (1, -1, 0):
+        at_distance(dz, first_push, dz != 0)
+    for n, distances in enumerate(((2,), (4, 3), (7, 6, 5))):
+        pl.semaphore_wait(ready.at[n], 2)
+        if n < 2:
+            widen(n + 1)
+        if n == 2:
+            for dy in range(ROWS_Y):
+                leg(0, dy).start()
+        for d in distances:
+            at_distance(d, first_push)
+            at_distance(-d, first_push)
+    for dy in range(ROWS_Y):
+        leg(1, dy).start()
+    each_peer(push(send.at[1], recv.at[1], send_sem.at[1], recv_sem.at[1]), 1)
+    for h in range(PAIR):
+        own_chunk(send.at[h], recv.at[h], own_sem.at[h]).start()
+
+    ahead.wait_recv()
     for dy in range(1, ROWS_Y):
-        @pl.when(y + dy < ROWS_Y)
+        @pl.when(y + dy >= ROWS_Y)
         def _(dy=dy):
             sideways(dy).start()
 
+    for h in range(PAIR):
+        legs(h).wait_recv()
+        onward(h).start()
+
     def routed(h):
         arrived(recv.at[h], send_sem.at[h], recv_sem.at[h]).wait_recv()
-        own_chunk(send.at[h], recv.at[h], own_sem.at[2 + h]).wait()
+        own_chunk(send.at[h], recv.at[h], own_sem.at[h]).wait()
         q, k, v = (
             recv[h, :, :, n * HD:(n + 1) * HD].astype(jnp.float32).reshape(SLOTS, HD).astype(jnp.bfloat16)
             for n in range(3)
@@ -149,14 +214,9 @@
             mixed = blend(jnp.where(allowed, scores, MASKED), v[:hi])
             osend[h, b * 16:(b + 1) * 16] = mixed.reshape(16, ROOM, HD).astype(jnp.bfloat16)
         each_peer(push(osend.at[h], home.at[h], osend_sem.at[h], home_sem.at[h]))
-        own_chunk(osend.at[h], home.at[h], own_sem.at[4 + h]).start()
+        own_chunk(osend.at[h], home.at[h], own_sem.at[2 + h]).start()
 
     routed(0)
-    ahead.wait_recv()
-    for dy in range(1, ROWS_Y):
-        @pl.when(y + dy >= ROWS_Y)
-        def _(dy=dy):
-            sideways(dy).start()
     routed(1)
 
     for dy in range(1, ROWS_Y):
@@ -177,12 +237,18 @@
     for h in range(PAIR):
         back = jnp.where(lax.broadcasted_iota(jnp.int32, (TOK, SLOTS), 1) == slot_cols[h], 1.0, 0.0).astype(jnp.bfloat16)
         arrived(home.at[h], osend_sem.at[h], home_sem.at[h]).wait_recv()
-        own_chunk(osend.at[h], home.at[h], own_sem.at[4 + h]).wait()
+        own_chunk(osend.at[h], home.at[h], own_sem.at[2 + h]).wait()
         rows = home[h].astype(jnp.float32).reshape(SLOTS, HD).astype(jnp.bfloat16)
         out_ref[:, SPLIT + h * HD:SPLIT + (h + 1) * HD] = dot(back, rows).astype(jnp.bfloat16)
 
     for h in range(PAIR):
-        arrived(recv.at[h], send_sem.at[h], recv_sem.at[h]).wait_send()
+        sent = send.at[h, pl.ds(0, SEQ - 1 - ROWS_Y)]
+        pltpu.make_async_remote_copy(
+            src_ref=sent, dst_ref=sent, send_sem=send_sem.at[h], recv_sem=recv_sem.at[h],
+            device_id={"seq": (me + 1) % SEQ},
+        ).wait_send()
+        legs(h).wait_send()
+        onward(h).wait_send()
         arrived(home.at[h], osend_sem.at[h], home_sem.at[h]).wait_send()
     ahead.wait_send()
     for dy in range(1, ROWS_Y):
@@ -194,26 +260,36 @@
     return pl.pallas_call(
         kernel,
         out_shape=jax.ShapeDtypeStruct(query_rows.shape, jnp.bfloat16),
-        in_specs=[vmem] * 5,
+        in_specs=[pl.BlockSpec(memory_space=pltpu.HBM)] * 4,
         out_specs=vmem,
         scratch_shapes=[
+            pltpu.VMEM((TOK, 2 * SPLIT), jnp.bfloat16),
+            pltpu.VMEM((TOK, 2 * SPLIT), jnp.bfloat16),
+            pltpu.VMEM((TOK, 2 * SPLIT), jnp.bfloat16),
+            pltpu.VMEM((PAIR, 1, TOK), jnp.int32),
             pltpu.VMEM((PAIR, SEQ, ROOM, 3 * HD), jnp.bfloat16),
             pltpu.VMEM((PAIR, SEQ, ROOM, 3 * HD), jnp.bfloat16),
             pltpu.VMEM((PAIR, SEQ, ROOM, HD), jnp.bfloat16),
             pltpu.VMEM((PAIR, SEQ, ROOM, HD), jnp.bfloat16),
             pltpu.VMEM((SPAN + 1, TOK, 2 * SPLIT), jnp.bfloat16),
+            pltpu.VMEM((PAIR, ROWS_Y, ROOM, 3 * HD), jnp.bfloat16),
             pltpu.SemaphoreType.DMA((6,)),
+            pltpu.SemaphoreType.DMA((4,)),
             pltpu.SemaphoreType.DMA((PAIR,)),
             pltpu.SemaphoreType.DMA((PAIR,)),
             pltpu.SemaphoreType.DMA((PAIR,)),
             pltpu.SemaphoreType.DMA((PAIR,)),
             pltpu.SemaphoreType.DMA((SPAN,)),
             pltpu.SemaphoreType.DMA((SPAN,)),
+            pltpu.SemaphoreType.REGULAR((3,)),
+            pltpu.SemaphoreType.DMA((PAIR,)),
+            pltpu.SemaphoreType.DMA((PAIR,)),
+            pltpu.SemaphoreType.DMA((PAIR,)),
         ],
         compiler_params=pltpu.CompilerParams(
-            collective_id=0, has_side_effects=True, vmem_limit_bytes=48 * 1024 * 1024
+            collective_id=0, has_side_effects=True, vmem_limit_bytes=67043328
         ),
-    )(query_rows, key_rows, value_rows, cluster_ids, cluster_ids[:, :, 0])
+    )(query_rows, key_rows, value_rows, cluster_ids.transpose(0, 2, 1))
 
 
 def solution(mesh):

time: 80 us -> 73.1 us (0.914); the launches traced: 78.9 us -> 72.9 us
  Pallas kernels: 75.3 us -> 71.2 us
  local copies, waits for them, and re-layouts: 3.58 us -> 1.67 us
    pallas_call x1, Pallas kernels: 75.3 us -> 71.2 us  [per_device(): pl.pallas_call(kernel, out_shape=jax.ShapeDtypeStruct(query_rows.shape, j...]
    unnamed x11 -> x1, local copies, waits for them, and re-layouts: 3.58 us -> 1.67 us
where the time goes in v2:
time: 73.1 us; the launch traced here: 72.9 us
  Pallas kernels  71.2 us (97%)
  local copies, waits for them, and re-layouts  1.67 us (2%)
    pallas_call x1, Pallas kernels, per_device(): pl.pallas_call(kernel, out_shape=jax.ShapeDtypeStruct(query_rows.shape, j...  71.2 us
    unnamed x1, local copies, waits for them, and re-layouts  1.67 us

profile of v2, /device:TPU:6, one launch (start us, length us, event | category | flops | bytes accessed | tf_op | source)
XLA Modules:
  0.0 72.9 jit_solution(3046270083736414457)
XLA Ops:
  0.0 71.2 %shard_map.46 = bf16[256,512]{1,0:T(8,128)(2,1)} custom-call(bf16[256,512]{1,0:T(8,128)(2,1)} %q_hbm.1, bf16[256,512]{1,0:T(8,128)(2,1)} %k_hbm.1, bf16[256,512]{1,0:T(8,128)(2,1)} %v_hbm.1, s32[2,1,256]{2,1,0:T(1,128)} %bitcast.1), custom_call_target="tpu_custom_call" | custom-call | tf_op jit(solution)/shard_map/pallas_call | solution.py:260
  71.2 1.7 %copy.6 = bf16[256,512]{1,0:T(8,128)(2,1)} copy(bf16[256,512]{1,0:T(8,128)(2,1)} %shard_map.46) | data formatting | bytes 524288

commit v3 on v2

--- a/solution.py
+++ b/solution.py
@@ -180,19 +180,19 @@
             at_distance(-d, first_push)
     for dy in range(ROWS_Y):
         leg(1, dy).start()
+    legs(0).wait_recv()
+    onward(0).start()
     each_peer(push(send.at[1], recv.at[1], send_sem.at[1], recv_sem.at[1]), 1)
     for h in range(PAIR):
         own_chunk(send.at[h], recv.at[h], own_sem.at[h]).start()
 
+    legs(1).wait_recv()
+    onward(1).start()
     ahead.wait_recv()
     for dy in range(1, ROWS_Y):
         @pl.when(y + dy >= ROWS_Y)
         def _(dy=dy):
             sideways(dy).start()
-
-    for h in range(PAIR):
-        legs(h).wait_recv()
-        onward(h).start()
 
     def routed(h):
         arrived(recv.at[h], send_sem.at[h], recv_sem.at[h]).wait_recv()

time: 73.1 us -> 70.4 us (0.963)
  Pallas kernels: 71.2 us -> 68.6 us
    pallas_call x1, Pallas kernels: 71.2 us -> 68.6 us  [per_device(): pl.pallas_call(kernel, out_shape=jax.ShapeDtypeStruct(query_rows.shape, j...]
where the time goes in v3:
time: 70.4 us; the launch traced here: 70.3 us
  Pallas kernels  68.6 us (97%)
  local copies, waits for them, and re-layouts  1.67 us (2%)
    pallas_call x1, Pallas kernels, per_device(): pl.pallas_call(kernel, out_shape=jax.ShapeDtypeStruct(query_rows.shape, j...  68.6 us
    unnamed x1, local copies, waits for them, and re-layouts  1.67 us

profile of v3, /device:TPU:6, one launch (start us, length us, event | category | flops | bytes accessed | tf_op | source)
XLA Modules:
  0.0 70.3 jit_solution(11610219126688959834)
XLA Ops:
  0.0 68.6 %shard_map.46 = bf16[256,512]{1,0:T(8,128)(2,1)} custom-call(bf16[256,512]{1,0:T(8,128)(2,1)} %q_hbm.1, bf16[256,512]{1,0:T(8,128)(2,1)} %k_hbm.1, bf16[256,512]{1,0:T(8,128)(2,1)} %v_hbm.1, s32[2,1,256]{2,1,0:T(1,128)} %bitcast.1), custom_call_target="tpu_custom_call" | custom-call | tf_op jit(solution)/shard_map/pallas_call | solution.py:260
  68.6 1.7 %copy.6 = bf16[256,512]{1,0:T(8,128)(2,1)} copy(bf16[256,512]{1,0:T(8,128)(2,1)} %shard_map.46) | data formatting | bytes 524288

commit v4 on v3

--- a/solution.py
+++ b/solution.py
@@ -180,6 +180,11 @@
             at_distance(-d, first_push)
     for dy in range(ROWS_Y):
         leg(1, dy).start()
+    ahead.wait_recv()
+    for dy in range(1, ROWS_Y):
+        @pl.when(y + dy >= ROWS_Y)
+        def _(dy=dy):
+            sideways(dy).start()
     legs(0).wait_recv()
     onward(0).start()
     each_peer(push(send.at[1], recv.at[1], send_sem.at[1], recv_sem.at[1]), 1)
@@ -188,12 +193,6 @@
 
     legs(1).wait_recv()
     onward(1).start()
-    ahead.wait_recv()
-    for dy in range(1, ROWS_Y):
-        @pl.when(y + dy >= ROWS_Y)
-        def _(dy=dy):
-            sideways(dy).start()
-
     def routed(h):
         arrived(recv.at[h], send_sem.at[h], recv_sem.at[h]).wait_recv()
         own_chunk(send.at[h], recv.at[h], own_sem.at[h]).wait()
@@ -217,8 +216,6 @@
         own_chunk(osend.at[h], home.at[h], own_sem.at[2 + h]).start()
 
     routed(0)
-    routed(1)
-
     for dy in range(1, ROWS_Y):
         sideways(dy).wait_recv()
     width = (SPAN + 1) * TOK
@@ -233,6 +230,8 @@
         scores = dot(q_ref[:, h * HD:(h + 1) * HD], k, NT) * scale
         mixed = blend(jnp.where(allowed, scores, MASKED), v)
         out_ref[:, h * HD:(h + 1) * HD] = mixed.astype(jnp.bfloat16)
+
+    routed(1)
 
     for h in range(PAIR):
         back = jnp.where(lax.broadcasted_iota(jnp.int32, (TOK, SLOTS), 1) == slot_cols[h], 1.0, 0.0).astype(jnp.bfloat16)

time: 70.4 us -> 70.6 us (level)
  no operation moved by 1% of the time
where the time goes in v4:
time: 70.6 us; the launch traced here: 70.5 us
  Pallas kernels  68.8 us (97%)
  local copies, waits for them, and re-layouts  1.67 us (2%)
    pallas_call x1, Pallas kernels, per_device(): pl.pallas_call(kernel, out_shape=jax.ShapeDtypeStruct(query_rows.shape, j...  68.8 us
    unnamed x1, local copies, waits for them, and re-layouts  1.67 us

profile of v4, /device:TPU:6, one launch (start us, length us, event | category | flops | bytes accessed | tf_op | source)
XLA Modules:
  0.0 70.5 jit_solution(14559982898043289766)
XLA Ops:
  0.0 68.8 %shard_map.46 = bf16[256,512]{1,0:T(8,128)(2,1)} custom-call(bf16[256,512]{1,0:T(8,128)(2,1)} %q_hbm.1, bf16[256,512]{1,0:T(8,128)(2,1)} %k_hbm.1, bf16[256,512]{1,0:T(8,128)(2,1)} %v_hbm.1, s32[2,1,256]{2,1,0:T(1,128)} %bitcast.1), custom_call_target="tpu_custom_call" | custom-call | tf_op jit(solution)/shard_map/pallas_call | solution.py:259
  68.8 1.7 %copy.6 = bf16[256,512]{1,0:T(8,128)(2,1)} copy(bf16[256,512]{1,0:T(8,128)(2,1)} %shard_map.46) | data formatting | bytes 524288
